TPU v7x, 32 devices: a whole 2x2x4 slice. The times are simulated.
32 devices in a mesh: grp: 4 (over y, core), row: 8 (over z, x).
Axes of the slice: x: 2, y: 2, z: 4, core: 2. Of those that a mesh axis runs over, the one named last changes fastest.
Arguments:
- labeled: bfloat16 [4, 1024, 1024], P(None, 'row', 'grp'), may hold values from -6 to 6
- candidates: bfloat16 [4096, 1024], P(('grp', 'row')), may hold values from -6 to 6
- factor_rows: bfloat16 [4, 1024, 4096], P(None, 'row'), may hold values from -6 to 6
- block_inverse: bfloat16 [4, 1024, 1024], P(None, 'row'), as said below
Outputs:
- whitened: bfloat16 [4, 1024, 4096], P(None, 'row', 'grp')
- explained: float32 [4096], P('grp')
Inputs may be any that keep to these rules, and one draw needn't show every extreme that they name: Each block of block_inverse is lower triangular with a positive diagonal; it is given as is and is not derived from factor_rows.
All inputs are finite; a program needn't handle non-finite values.
Results may differ from a plain program's by a relative error of at most 0.0075.
Values may be sent and summed in bfloat16 or wider, within the bound.
No kernel may reach another device: no remote copies, remote signals or barrier semaphores. Data moves between devices by JAX's collectives and lax.ppermute only.
A program may use at most 64 MiB of HBM per device.

v0:
```python
import math
import jax
import jax.numpy as jnp
from jax import lax
from jax.sharding import PartitionSpec as P


def on_device(labeled, candidates, factor_rows, block_inverse):
    gathered = lax.all_gather(labeled, "grp", axis=2, tiled=True)
    block_count = gathered.shape[0]
    own_count = gathered.shape[1]
    feature_width = gathered.shape[2]
    block_size = block_inverse.shape[2]
    kernel_scale = 0.5 / math.sqrt(feature_width)
    flat_rows = gathered.reshape(block_count * own_count, feature_width)
    kernel = jnp.exp(
        jnp.dot(
            flat_rows,
            lax.all_gather(candidates, "row", axis=0, tiled=True).T,
            preferred_element_type=jnp.float32,
        )
        * kernel_scale
    )
    cand_count = kernel.shape[1]
    kernel = kernel.reshape(block_count, own_count, cand_count)
    pending = [kernel[number] for number in range(block_count)]
    solved_own = []
    for number in range(block_count):
        rounded = pending[number].astype(jnp.bfloat16)
        residual_block = lax.all_gather(rounded, "row", axis=0, tiled=True)
        own_rows = jnp.dot(
            block_inverse[number], residual_block, preferred_element_type=jnp.float32
        ).astype(jnp.bfloat16)
        solved = lax.all_gather(own_rows, "row", axis=0, tiled=True)
        solved_own.append(own_rows)
        lower_edge = number * block_size
        upper_edge = (number + 1) * block_size
        if number + 1 < block_count:
            panel = factor_rows[number + 1 :, :, lower_edge:upper_edge]
            later_count = block_count - number - 1
            updates = jnp.dot(
                panel.reshape(later_count * own_count, block_size),
                solved,
                preferred_element_type=jnp.float32,
            )
            updates = updates.reshape(later_count, own_count, cand_count)
            for later in range(later_count):
                pending[number + 1 + later] = pending[number + 1 + later] - updates[later]
    whitened = jnp.stack(solved_own, axis=0)
    squares = jnp.sum(jnp.square(whitened.astype(jnp.float32)), axis=(0, 1))
    explained = lax.psum(squares, "row")
    return (whitened, explained)


def solution(mesh):
    in_specs = (
        P(None, "row", "grp"),
        P(("grp", "row"), None),
        P(None, "row", None),
        P(None, "row", None),
    )
    out_specs = (P(None, "row", "grp"), P("grp"))
    return jax.shard_map(
        on_device, mesh=mesh, in_specs=in_specs, out_specs=out_specs, check_vma=False
    )
```

profile of v0, /device:TPU:0, one launch (start us, length us, event | category | flops | bytes accessed | tf_op | source)
XLA Modules:
  0.0 468.7 jit_solution(2871599879833106389)
XLA Ops:
  7.2 0.7 all-gather.10.cloned.1.call-update
  7.9 0.7 all-gather.12.cloned.1.call-update
  8.7 20.4 %all-gather.10.cloned.1.call-done = bf16[4,128,1024]{2,1,0:T(8,128)(2,1)} async-done(((bf16[4,128,256]{2,1,0:T(8,128)(2,1)}), bf16[4,128,1024]{2,1,0:T(8,128)(2,1)}) %all-gather.10.cloned.1.call-update) | async-done | bytes 1048592 | tf_op jit(solution)/shard_map/all_gather | solution.py:9
  29.1 51.2 %all-gather.12.cloned.1.call-done = bf16[1024,1024]{1,0:T(8,128)(2,1)} async-done(((bf16[128,1024]{1,0:T(8,128)(2,1)}), bf16[1024,1024]{1,0:T(8,128)(2,1)}) %all-gather.12.cloned.1.call-update) | async-done | bytes 2097168 | tf_op jit(solution)/shard_map/all_gather | solution.py:19
  80.3 3.3 multiply_exponential_fusion
  83.7 0.8 slice.122
  84.5 0.0 all-gather.16.cloned.1.call-start
  84.5 47.7 %all-gather.14.cloned.1.call-done = bf16[1024,1024]{1,0:T(8,128)(2,1)} async-done(((bf16[128,1024]{1,0:T(8,128)(2,1)}), bf16[1024,1024]{1,0:T(8,128)(2,1)}) %all-gather.14.cloned.1.call-update) | async-done | bytes 2097168 | tf_op jit(solution)/shard_map/all_gather | solution.py:30
  132.3 2.7 convolution_convert_fusion.3
  135.0 0.0 all-gather.18.cloned.1.call-start
  135.1 2.1 slice.61
  137.1 45.7 %all-gather.16.cloned.1.call-done = bf16[1024,1024]{1,0:T(8,128)(2,1)} async-done(((bf16[128,1024]{1,0:T(8,128)(2,1)}), bf16[1024,1024]{1,0:T(8,128)(2,1)}) %all-gather.16.cloned.1.call-update) | async-done | bytes 2097168 | tf_op jit(solution)/shard_map/all_gather | solution.py:34
  182.8 2.8 convolution_bitcast_fusion
  185.6 1.2 copy-done.4
  186.8 0.8 fusion.4
  187.6 0.0 all-gather.20.cloned.1.call-start
  187.6 47.7 %all-gather.18.cloned.1.call-done = bf16[1024,1024]{1,0:T(8,128)(2,1)} async-done(((bf16[128,1024]{1,0:T(8,128)(2,1)}), bf16[1024,1024]{1,0:T(8,128)(2,1)}) %all-gather.18.cloned.1.call-update) | async-done | bytes 2097168 | tf_op jit(solution)/shard_map/all_gather | solution.py:30
  235.4 2.7 convolution_convert_fusion.2
  238.1 0.0 all-gather.22.cloned.1.call-start
  238.2 1.1 slice.66
  239.3 46.6 %all-gather.20.cloned.1.call-done = bf16[1024,1024]{1,0:T(8,128)(2,1)} async-done(((bf16[128,1024]{1,0:T(8,128)(2,1)}), bf16[1024,1024]{1,0:T(8,128)(2,1)}) %all-gather.20.cloned.1.call-update) | async-done | bytes 2097168 | tf_op jit(solution)/shard_map/all_gather | solution.py:34
  285.9 2.3 convolution_bitcast_fusion.1
  288.2 1.8 fusion.3
  290.1 0.0 all-gather.24.cloned.1.call-start
  290.1 47.7 %all-gather.22.cloned.1.call-done = bf16[1024,1024]{1,0:T(8,128)(2,1)} async-done(((bf16[128,1024]{1,0:T(8,128)(2,1)}), bf16[1024,1024]{1,0:T(8,128)(2,1)}) %all-gather.22.cloned.1.call-update) | async-done | bytes 2097168 | tf_op jit(solution)/shard_map/all_gather | solution.py:30
  337.8 2.8 convolution_convert_fusion.1
  340.8 47.7 %all-gather.24.cloned.1.call-done = bf16[1024,1024]{1,0:T(8,128)(2,1)} async-done(((bf16[128,1024]{1,0:T(8,128)(2,1)}), bf16[1024,1024]{1,0:T(8,128)(2,1)}) %all-gather.24.cloned.1.call-update) | async-done | bytes 2097168 | tf_op jit(solution)/shard_map/all_gather | solution.py:34
  388.5 2.9 fusion.1
  391.4 47.8 %all-gather.26.cloned.1.call-done = bf16[1024,1024]{1,0:T(8,128)(2,1)} async-done(((bf16[128,1024]{1,0:T(8,128)(2,1)}), bf16[1024,1024]{1,0:T(8,128)(2,1)}) %all-gather.26.cloned.1.call-update) | async-done | bytes 2097168 | tf_op jit(solution)/shard_map/all_gather | solution.py:30
  439.2 2.1 fusion.2
  441.4 1.3 multiply_reduce_fusion
  442.6 19.5 %psum.7 = f32[1024]{0:T(1024)} all-reduce(f32[1024]{0:T(1024)S(1)} %get-tuple-element.2), channel_id=1, replica_groups=mesh['grp'=4,'row'=8] {'row'}, use_global_device_ids=true, to_apply=%region_1.0 | all-reduce | flops 1024 | bytes 8192 | tf_op jit(solution)/shard_map/psum | solution.py:51
  (24 shorter events, 0.3 us)
Async XLA Ops:
  7.2 21.9 %all-gather.10.cloned.1.call-start = ((), (), s32[]{:S(2)}) async-start(), calls=%async_computation | async-start | bytes 1310720 | tf_op jit(solution)/shard_map/all_gather | solution.py:9
  7.9 72.4 %all-gather.12.cloned.1.call-start = ((), (), s32[]{:S(2)}) async-start(), calls=%async_computation.1 | async-start | bytes 2359296 | tf_op jit(solution)/shard_map/all_gather | solution.py:19
  8.6 123.6 %all-gather.14.cloned.1.call-start = ((), (), s32[]{:S(2)}) async-start(), calls=%async_computation.2 | async-start | bytes 2359296 | tf_op jit(solution)/shard_map/all_gather | solution.py:30
  80.3 51.9 %copy-start.6 = (bf16[4,128,1024]{2,1,0:T(8,128)(2,1)S(1)}, bf16[4,128,1024]{2,1,0:T(8,128)(2,1)}, u32[]{:S(2)}) copy-start(bf16[4,128,1024]{2,1,0:T(8,128)(2,1)} %param.7) | copy-start | bytes 3145732
  83.7 102.0 %copy-start.3 = (f32[512,1024]{1,0:T(8,128)}, f32[512,1024]{1,0:T(8,128)S(1)}, u32[]{:S(2)}) copy-start(f32[512,1024]{1,0:T(8,128)S(1)} %multiply_exponential_fusion) | copy-start | bytes 6291460
  84.5 98.3 %all-gather.16.cloned.1.call-start = ((), (), s32[]{:S(2)}) async-start(), calls=%async_computation.3 | async-start | bytes 2359296 | tf_op jit(solution)/shard_map/all_gather | solution.py:34
  135.0 100.3 %all-gather.18.cloned.1.call-start = ((), (), s32[]{:S(2)}) async-start(), calls=%async_computation.4 | async-start | bytes 2359296 | tf_op jit(solution)/shard_map/all_gather | solution.py:30
  185.6 1.2 copy-start.4
  187.6 98.3 %all-gather.20.cloned.1.call-start = ((), (), s32[]{:S(2)}) async-start(), calls=%async_computation.5 | async-start | bytes 2359296 | tf_op jit(solution)/shard_map/all_gather | solution.py:34
  238.1 99.7 %all-gather.22.cloned.1.call-start = ((), (), s32[]{:S(2)}) async-start(), calls=%async_computation.6 | async-start | bytes 2359296 | tf_op jit(solution)/shard_map/all_gather | solution.py:30
  239.3 48.9 %copy-start.5 = (f32[384,1024]{1,0:T(8,128)S(1)}, f32[384,1024]{1,0:T(8,128)}, u32[]{:S(2)}) copy-start(f32[384,1024]{1,0:T(8,128)} %copy-done.4) | copy-start | bytes 4718596
  290.1 98.4 %all-gather.24.cloned.1.call-start = ((), (), s32[]{:S(2)}) async-start(), calls=%async_computation.7 | async-start | bytes 2359296 | tf_op jit(solution)/shard_map/all_gather | solution.py:34
  340.7 98.5 %all-gather.26.cloned.1.call-start = ((), (), s32[]{:S(2)}) async-start(), calls=%async_computation.8 | async-start | bytes 2359296 | tf_op jit(solution)/shard_map/all_gather | solution.py:30
  391.4 49.9 %copy-start = (bf16[1024,128]{0,1:T(8,128)(2,1)S(1)}, bf16[1024,128]{0,1:T(8,128)(2,1)}, u32[]{:S(2)}) copy-start(bf16[1024,128]{0,1:T(8,128)(2,1)} %convolution_convert_fusion.3) | copy-start | bytes 786436
  391.4 50.0 %copy-start.1 = (bf16[1024,128]{0,1:T(8,128)(2,1)S(1)}, bf16[1024,128]{0,1:T(8,128)(2,1)}, u32[]{:S(2)}) copy-start(bf16[1024,128]{0,1:T(8,128)(2,1)} %convolution_convert_fusion.2) | copy-start | bytes 786436
  391.4 50.0 %copy-start.2 = (bf16[1024,128]{0,1:T(8,128)(2,1)S(1)}, bf16[1024,128]{0,1:T(8,128)(2,1)}, u32[]{:S(2)}) copy-start(bf16[1024,128]{0,1:T(8,128)(2,1)} %convolution_convert_fusion.1) | copy-start | bytes 786436
Sparse Core Ops, SparseCore 0:
  9.5 19.5 all-gather.9
  31.2 49.0 all-gather.11
  84.6 47.6 all-gather.13
  135.1 47.6 all-gather.15
  187.7 47.6 all-gather.17
  238.2 47.6 all-gather.19
  290.2 47.6 all-gather.21
  340.8 47.6 all-gather.23
  391.6 47.6 all-gather.25
where the time goes:
time: 469 us
  waiting for transfers between devices  404 us (86%)
  matrix products  21.8 us (5%)
  blocking collectives  19.5 us (4%)
  between operations  13.9 us (3%)
  local copies, waits for them, and re-layouts  5.13 us (1%)
    all_gather x4, waiting for transfers between devices, on_device(): residual_block = lax.all_gather(rounded, 'row', axis=0, tiled=True)  191 us
    all_gather x3, waiting for transfers between devices, on_device(): solved = lax.all_gather(own_rows, 'row', axis=0, tiled=True)  140 us
    all_gather x1, waiting for transfers between devices, on_device(): lax.all_gather(candidates, 'row', axis=0, tiled=True)  51.2 us
    all_gather x1, waiting for transfers between devices, on_device(): gathered = lax.all_gather(labeled, 'grp', axis=2, tiled=True)  20.4 us
    psum x1, blocking collectives, on_device(): explained = lax.psum(squares, 'row')  19.5 us
    dot_general x4, matrix products, on_device(): jnp.dot(block_inverse[number], residual_block, preferred_element_type=jnp...  10.4 us
  transfers between devices with their start and end apart: 9, of which 9 were waited for; matrix products, arithmetic and copies ran while one was open for 1% of the time, Pallas kernels for 0%

commit v1 on v0

--- a/solution.py
+++ b/solution.py
@@ -31,7 +31,16 @@
         own_rows = jnp.dot(
             block_inverse[number], residual_block, preferred_element_type=jnp.float32
         ).astype(jnp.bfloat16)
-        solved = lax.all_gather(own_rows, "row", axis=0, tiled=True)
+        response, state_next = (lax.axis_size("row"), lax.axis_index("row"))
+        solved, met_up = (own_rows, 1)
+        while met_up < response:
+            extra = lax.ppermute(
+                solved, "row", tuple(((dev_j, dev_j ^ met_up) for dev_j in range(response)))
+            )
+            u1 = jnp.concatenate([solved, extra], 0)
+            current_block = jnp.concatenate([extra, solved], axis=0)
+            solved = jnp.where(state_next & met_up == 0, u1, current_block)
+            met_up = 2 * met_up
         solved_own.append(own_rows)
         lower_edge = number * block_size
         upper_edge = (number + 1) * block_size

time: 469 us -> 525 us (1.12)
  waiting for transfers between devices: 404 us -> 443 us
  starting transfers between devices: 0.37 us -> 17.2 us
    ppermute x0 -> x9, waiting for transfers between devices: none -> 175 us  [on_device(): lax.ppermute(solved, 'row', tuple(((dev_j, dev_j ^ met_up) for dev_j in r...]
    all_gather x3 -> x0, waiting for transfers between devices: 140 us -> none  [on_device(): solved = lax.all_gather(own_rows, 'row', axis=0, tiled=True)]
    ppermute x0 -> x9, starting transfers between devices: none -> 16.9 us  [on_device(): lax.ppermute(solved, 'row', tuple(((dev_j, dev_j ^ met_up) for dev_j in r...]
  transfers between devices with their start and end apart: 9 -> 15, of which waited for: 9 -> 15; matrix products, arithmetic and copies ran while one was open for 1% -> 0% of each run, Pallas kernels for 0% -> 0%
where the time goes in v1:
time: 525 us; the launch traced here: 524 us
  waiting for transfers between devices  443 us (84%)
  blocking collectives  19.5 us (4%)
  matrix products  17.6 us (3%)
  starting transfers between devices  17.2 us (3%)
  between operations  14.3 us (3%)
  other arithmetic  6.75 us (1%)
  local copies, waits for them, and re-layouts  6.48 us (1%)
    all_gather x4, waiting for transfers between devices, on_device(): residual_block = lax.all_gather(rounded, 'row', axis=0, tiled=True)  195 us
    ppermute x9, waiting for transfers between devices, on_device(): lax.ppermute(solved, 'row', tuple(((dev_j, dev_j ^ met_up) for dev_j in r...  175 us
    all_gather x1, waiting for transfers between devices, on_device(): lax.all_gather(candidates, 'row', axis=0, tiled=True)  51.2 us
    all_gather x1, waiting for transfers between devices, on_device(): gathered = lax.all_gather(labeled, 'grp', axis=2, tiled=True)  20.4 us
    psum x1, blocking collectives, on_device(): explained = lax.psum(squares, 'row')  19.5 us
    ppermute x9, starting transfers between devices, on_device(): lax.ppermute(solved, 'row', tuple(((dev_j, dev_j ^ met_up) for dev_j in r...  16.9 us
  transfers between devices with their start and end apart: 15, of which 15 were waited for; matrix products, arithmetic and copies ran while one was open for 0% of the time, Pallas kernels for 0%

profile of v1, /device:TPU:0, one launch (start us, length us, event | category | flops | bytes accessed | tf_op | source)
XLA Modules:
  0.0 524.4 jit_solution(2352394604683688092)
XLA Ops:
  8.7 20.4 %all-gather.7.cloned.1.call-done = bf16[4,128,1024]{2,1,0:T(8,128)(2,1)} async-done(((bf16[4,128,256]{2,1,0:T(8,128)(2,1)}), bf16[4,128,1024]{2,1,0:T(8,128)(2,1)}) %all-gather.7.cloned.1.call-update) | async-done | bytes 1048592 | tf_op jit(solution)/shard_map/all_gather | solution.py:9
  29.1 51.2 %all-gather.9.cloned.1.call-done = bf16[1024,1024]{1,0:T(8,128)(2,1)} async-done(((bf16[128,1024]{1,0:T(8,128)(2,1)}), bf16[1024,1024]{1,0:T(8,128)(2,1)}) %all-gather.9.cloned.1.call-update) | async-done | bytes 2097168 | tf_op jit(solution)/shard_map/all_gather | solution.py:19
  80.3 3.3 multiply_exponential_fusion
  83.7 1.3 copy-done.1
  85.8 47.7 %all-gather.11.cloned.1.call-done = bf16[1024,1024]{1,0:T(8,128)(2,1)} async-done(((bf16[128,1024]{1,0:T(8,128)(2,1)}), bf16[1024,1024]{1,0:T(8,128)(2,1)}) %all-gather.11.cloned.1.call-update) | async-done | bytes 2097168 | tf_op jit(solution)/shard_map/all_gather | solution.py:30
  133.5 2.0 convolution_convert_fusion.3
  136.2 5.8 %collective-permute-done = bf16[128,1024]{1,0:T(8,128)(2,1)S(1)} collective-permute-done((bf16[128,1024]{1,0:T(8,128)(2,1)S(1)}, bf16[128,1024]{1,0:T(8,128)(2,1)S(1)}, u32[]{:S(2)}, u32[]{:S(2)}) %collective-permute-start) | collective-permute-done | bytes 262176 | tf_op jit(solution)/shard_map/ppermute | solution.py:37
  142.2 2.2 collective-permute-start.1
  144.3 10.0 %collective-permute-done.1 = bf16[256,1024]{1,0:T(8,128)(2,1)S(1)} collective-permute-done((bf16[256,1024]{1,0:T(8,128)(2,1)S(1)}, bf16[256,1024]{1,0:T(8,128)(2,1)S(1)}, u32[]{:S(2)}, u32[]{:S(2)}) %collective-permute-start.1) | collective-permute-done | bytes 524320 | tf_op jit(solution)/shard_map/ppermute | solution.py:37
  154.8 2.8 collective-permute-start.2
  158.8 42.1 %collective-permute-done.2 = bf16[512,1024]{1,0:T(8,128)(2,1)} collective-permute-done((bf16[512,1024]{1,0:T(8,128)(2,1)S(1)}, bf16[512,1024]{1,0:T(8,128)(2,1)}, u32[]{:S(2)}, u32[]{:S(2)}) %collective-permute-start.2) | collective-permute-done | bytes 1048608 | tf_op jit(solution)/shard_map/ppermute | solution.py:37
  201.0 2.6 fusion.21
  204.7 1.8 fusion.28
  206.6 49.0 %all-gather.13.cloned.1.call-done = bf16[1024,1024]{1,0:T(8,128)(2,1)} async-done(((bf16[128,1024]{1,0:T(8,128)(2,1)}), bf16[1024,1024]{1,0:T(8,128)(2,1)}) %all-gather.13.cloned.1.call-update) | async-done | bytes 2097168 | tf_op jit(solution)/shard_map/all_gather | solution.py:30
  255.6 2.0 convolution_convert_fusion.2
  258.2 5.8 %collective-permute-done.3 = bf16[128,1024]{1,0:T(8,128)(2,1)S(1)} collective-permute-done((bf16[128,1024]{1,0:T(8,128)(2,1)S(1)}, bf16[128,1024]{1,0:T(8,128)(2,1)S(1)}, u32[]{:S(2)}, u32[]{:S(2)}) %collective-permute-start.3) | collective-permute-done | bytes 262176 | tf_op jit(solution)/shard_map/ppermute | solution.py:37
  264.2 2.2 collective-permute-start.4
  266.4 10.0 %collective-permute-done.4 = bf16[256,1024]{1,0:T(8,128)(2,1)S(1)} collective-permute-done((bf16[256,1024]{1,0:T(8,128)(2,1)S(1)}, bf16[256,1024]{1,0:T(8,128)(2,1)S(1)}, u32[]{:S(2)}, u32[]{:S(2)}) %collective-permute-start.4) | collective-permute-done | bytes 524320 | tf_op jit(solution)/shard_map/ppermute | solution.py:37
  276.9 2.8 collective-permute-start.5
  280.8 42.1 %collective-permute-done.5 = bf16[512,1024]{1,0:T(8,128)(2,1)S(1)} collective-permute-done((bf16[512,1024]{1,0:T(8,128)(2,1)S(1)}, bf16[512,1024]{1,0:T(8,128)(2,1)S(1)}, u32[]{:S(2)}, u32[]{:S(2)}) %collective-permute-start.5) | collective-permute-done | bytes 1048608 | tf_op jit(solution)/shard_map/ppermute | solution.py:37
  324.9 1.9 fusion.27
  326.8 49.0 %all-gather.15.cloned.1.call-done = bf16[1024,1024]{1,0:T(8,128)(2,1)} async-done(((bf16[128,1024]{1,0:T(8,128)(2,1)}), bf16[1024,1024]{1,0:T(8,128)(2,1)}) %all-gather.15.cloned.1.call-update) | async-done | bytes 2097168 | tf_op jit(solution)/shard_map/all_gather | solution.py:30
  375.8 2.0 convolution_convert_fusion.1
  378.4 5.8 %collective-permute-done.6 = bf16[128,1024]{1,0:T(8,128)(2,1)S(1)} collective-permute-done((bf16[128,1024]{1,0:T(8,128)(2,1)S(1)}, bf16[128,1024]{1,0:T(8,128)(2,1)S(1)}, u32[]{:S(2)}, u32[]{:S(2)}) %collective-permute-start.6) | collective-permute-done | bytes 262176 | tf_op jit(solution)/shard_map/ppermute | solution.py:37
  384.4 2.2 collective-permute-start.7
  386.6 10.0 %collective-permute-done.7 = bf16[256,1024]{1,0:T(8,128)(2,1)S(1)} collective-permute-done((bf16[256,1024]{1,0:T(8,128)(2,1)S(1)}, bf16[256,1024]{1,0:T(8,128)(2,1)S(1)}, u32[]{:S(2)}, u32[]{:S(2)}) %collective-permute-start.7) | collective-permute-done | bytes 524320 | tf_op jit(solution)/shard_map/ppermute | solution.py:37
  397.1 2.8 collective-permute-start.8
  399.9 43.2 %collective-permute-done.8 = bf16[512,1024]{1,0:T(8,128)(2,1)S(1)} collective-permute-done((bf16[512,1024]{1,0:T(8,128)(2,1)S(1)}, bf16[512,1024]{1,0:T(8,128)(2,1)S(1)}, u32[]{:S(2)}, u32[]{:S(2)}) %collective-permute-start.8) | collective-permute-done | bytes 1048608 | tf_op jit(solution)/shard_map/ppermute | solution.py:37
  443.1 2.6 fusion.26
  445.7 49.0 %all-gather.17.cloned.1.call-done = bf16[1024,1024]{1,0:T(8,128)(2,1)} async-done(((bf16[128,1024]{1,0:T(8,128)(2,1)}), bf16[1024,1024]{1,0:T(8,128)(2,1)}) %all-gather.17.cloned.1.call-update) | async-done | bytes 2097168 | tf_op jit(solution)/shard_map/all_gather | solution.py:30
  494.7 2.0 fusion.24
  498.0 19.5 %psum.7 = f32[1024]{0:T(1024)} all-reduce(f32[1024]{0:T(1024)S(1)} %get-tuple-element.2), channel_id=1, replica_groups=mesh['grp'=4,'row'=8] {'row'}, use_global_device_ids=true, to_apply=%region_1.2 | all-reduce | flops 1024 | bytes 8192 | tf_op jit(solution)/shard_map/psum | solution.py:60
  (37 shorter events, 12.7 us)
Async XLA Ops:
  7.2 21.9 %all-gather.7.cloned.1.call-start = ((), (), s32[]{:S(2)}) async-start(), calls=%async_computation | async-start | bytes 1310720 | tf_op jit(solution)/shard_map/all_gather | solution.py:9
  7.9 72.4 %all-gather.9.cloned.1.call-start = ((), (), s32[]{:S(2)}) async-start(), calls=%async_computation.1 | async-start | bytes 2359296 | tf_op jit(solution)/shard_map/all_gather | solution.py:19
  8.6 124.9 %all-gather.11.cloned.1.call-start = ((), (), s32[]{:S(2)}) async-start(), calls=%async_computation.2 | async-start | bytes 2359296 | tf_op jit(solution)/shard_map/all_gather | solution.py:30
  80.3 53.2 %copy-start = (bf16[4,128,1024]{2,1,0:T(8,128)(2,1)S(1)}, bf16[4,128,1024]{2,1,0:T(8,128)(2,1)}, u32[]{:S(2)}) copy-start(bf16[4,128,1024]{2,1,0:T(8,128)(2,1)} %param.7) | copy-start | bytes 3145732
  83.7 1.3 copy-start.1
  85.8 169.8 %all-gather.13.cloned.1.call-start = ((), (), s32[]{:S(2)}) async-start(), calls=%async_computation.3 | async-start | bytes 2359296 | tf_op jit(solution)/shard_map/all_gather | solution.py:30
  135.6 6.4 %collective-permute-start = (bf16[128,1024]{1,0:T(8,128)(2,1)S(1)}, bf16[128,1024]{1,0:T(8,128)(2,1)S(1)}, u32[]{:S(2)}, u32[]{:S(2)}) collective-permute-start(bf16[128,1024]{1,0:T(8,128)(2,1)S(1)} %bitcast.49), channel_id=1, source_target_pairs={{0,1},{1,0},{2,3},{3,2},{4,5},{5,4},{6,7},{7,6},{8,9},{9,8},{10,11... | collective-permute-start | bytes 786440 | tf_op jit(solution)/shard_map/ppermute | solution.py:37
  142.2 12.2 %collective-permute-start.1 = (bf16[256,1024]{1,0:T(8,128)(2,1)S(1)}, bf16[256,1024]{1,0:T(8,128)(2,1)S(1)}, u32[]{:S(2)}, u32[]{:S(2)}) collective-permute-start(bf16[256,1024]{1,0:T(8,128)(2,1)S(1)} %maximum_select_fusion.15), channel_id=1, source_target_pairs={{0,2},{1,3},{2,0},{3,1},{4,6},{5,7},{6,4},{7,5},{8,10},{9,11},{10,... | collective-permute-start | bytes 1572872 | tf_op jit(solution)/shard_map/ppermute | solution.py:37
  154.8 46.1 %collective-permute-start.2 = (bf16[512,1024]{1,0:T(8,128)(2,1)S(1)}, bf16[512,1024]{1,0:T(8,128)(2,1)}, u32[]{:S(2)}, u32[]{:S(2)}) collective-permute-start(bf16[512,1024]{1,0:T(8,128)(2,1)S(1)} %maximum_select_fusion.12), channel_id=1, source_target_pairs={{0,4},{1,5},{2,6},{3,7},{4,0},{5,1},{6,2},{7,3},{8,12},{9,13},{10,... | collective-permute-start | bytes 3145736 | tf_op jit(solution)/shard_map/ppermute | solution.py:37
  203.5 1.2 copy-start.2
  206.5 169.2 %all-gather.15.cloned.1.call-start = ((), (), s32[]{:S(2)}) async-start(), calls=%async_computation.4 | async-start | bytes 2359296 | tf_op jit(solution)/shard_map/all_gather | solution.py:30
  257.6 6.4 %collective-permute-start.3 = (bf16[128,1024]{1,0:T(8,128)(2,1)S(1)}, bf16[128,1024]{1,0:T(8,128)(2,1)S(1)}, u32[]{:S(2)}, u32[]{:S(2)}) collective-permute-start(bf16[128,1024]{1,0:T(8,128)(2,1)S(1)} %bitcast.52), channel_id=1, source_target_pairs={{0,1},{1,0},{2,3},{3,2},{4,5},{5,4},{6,7},{7,6},{8,9},{9,8},{10,11... | collective-permute-start | bytes 786440 | tf_op jit(solution)/shard_map/ppermute | solution.py:37
  264.2 12.2 %collective-permute-start.4 = (bf16[256,1024]{1,0:T(8,128)(2,1)S(1)}, bf16[256,1024]{1,0:T(8,128)(2,1)S(1)}, u32[]{:S(2)}, u32[]{:S(2)}) collective-permute-start(bf16[256,1024]{1,0:T(8,128)(2,1)S(1)} %maximum_select_fusion.16), channel_id=1, source_target_pairs={{0,2},{1,3},{2,0},{3,1},{4,6},{5,7},{6,4},{7,5},{8,10},{9,11},{10,... | collective-permute-start | bytes 1572872 | tf_op jit(solution)/shard_map/ppermute | solution.py:37
  276.9 46.0 %collective-permute-start.5 = (bf16[512,1024]{1,0:T(8,128)(2,1)S(1)}, bf16[512,1024]{1,0:T(8,128)(2,1)S(1)}, u32[]{:S(2)}, u32[]{:S(2)}) collective-permute-start(bf16[512,1024]{1,0:T(8,128)(2,1)S(1)} %maximum_select_fusion.13), channel_id=1, source_target_pairs={{0,4},{1,5},{2,6},{3,7},{4,0},{5,1},{6,2},{7,3},{8,12},{9,13},{10,... | collective-permute-start | bytes 3145736 | tf_op jit(solution)/shard_map/ppermute | solution.py:37
  322.9 2.0 copy-start.3
  323.9 1.0 copy-start.4
  326.7 168.0 %all-gather.17.cloned.1.call-start = ((), (), s32[]{:S(2)}) async-start(), calls=%async_computation.5 | async-start | bytes 2359296 | tf_op jit(solution)/shard_map/all_gather | solution.py:30
  377.8 65.3 %copy-start.5 = (f32[256,1024]{1,0:T(8,128)S(1)}, f32[256,1024]{1,0:T(8,128)}, u32[]{:S(2)}) copy-start(f32[256,1024]{1,0:T(8,128)} %copy-done.4) | copy-start | bytes 3145732
  377.8 6.4 %collective-permute-start.6 = (bf16[128,1024]{1,0:T(8,128)(2,1)S(1)}, bf16[128,1024]{1,0:T(8,128)(2,1)S(1)}, u32[]{:S(2)}, u32[]{:S(2)}) collective-permute-start(bf16[128,1024]{1,0:T(8,128)(2,1)S(1)} %bitcast.55), channel_id=1, source_target_pairs={{0,1},{1,0},{2,3},{3,2},{4,5},{5,4},{6,7},{7,6},{8,9},{9,8},{10,11... | collective-permute-start | bytes 786440 | tf_op jit(solution)/shard_map/ppermute | solution.py:37
  384.4 12.2 %collective-permute-start.7 = (bf16[256,1024]{1,0:T(8,128)(2,1)S(1)}, bf16[256,1024]{1,0:T(8,128)(2,1)S(1)}, u32[]{:S(2)}, u32[]{:S(2)}) collective-permute-start(bf16[256,1024]{1,0:T(8,128)(2,1)S(1)} %maximum_select_fusion.17), channel_id=1, source_target_pairs={{0,2},{1,3},{2,0},{3,1},{4,6},{5,7},{6,4},{7,5},{8,10},{9,11},{10,... | collective-permute-start | bytes 1572872 | tf_op jit(solution)/shard_map/ppermute | solution.py:37
  397.1 46.0 %collective-permute-start.8 = (bf16[512,1024]{1,0:T(8,128)(2,1)S(1)}, bf16[512,1024]{1,0:T(8,128)(2,1)S(1)}, u32[]{:S(2)}, u32[]{:S(2)}) collective-permute-start(bf16[512,1024]{1,0:T(8,128)(2,1)S(1)} %maximum_select_fusion.14), channel_id=1, source_target_pairs={{0,4},{1,5},{2,6},{3,7},{4,0},{5,1},{6,2},{7,3},{8,12},{9,13},{10,... | collective-permute-start | bytes 3145736 | tf_op jit(solution)/shard_map/ppermute | solution.py:37
Sparse Core Ops, SparseCore 0:
  9.5 19.5 all-gather.6
  31.2 49.0 all-gather.8
  85.9 47.6 all-gather.10
  206.7 48.8 all-gather.12
  326.9 48.8 all-gather.14
  445.8 48.8 all-gather.16
